TPU v7x, 128 devices: a whole 4x4x4 slice. The times are simulated.
128 devices in a mesh: seq: 4 (over x), tp: 32 (over z, y, core).
Axes of the slice: x: 4, y: 4, z: 4, core: 2. Of those that a mesh axis runs over, the one named last changes fastest.
Arguments:
- hidden_in: bfloat16 [96, 4, 1024], P('tp'), may hold values from -6 to 6
- new_query: bfloat16 [96, 4, 1024], P('tp'), may hold values from -70 to 70
- new_key: bfloat16 [96, 4, 1024], P('tp'), may hold values from -15 to 15
- new_value: bfloat16 [96, 4, 1024], P('tp'), may hold values from -6 to 6
- key_cache: bfloat16 [96, 4096, 1024], P('tp', 'seq'), may hold values from -16 to 16
- value_cache: bfloat16 [96, 4096, 1024], P('tp', 'seq'), may hold values from -6 to 6
- lengths: int32 [96], P('tp'), may hold values from 64 to 4096, as said below
- out_weight: bfloat16 [1024, 1024], replicated, may hold values from -0.1875 to 0.1875
- norm_gain: float32 [1024], replicated, may hold values from 0.5 to 1.5
- router_weight: bfloat16 [1024, 16], replicated, may hold values from -0.1875 to 0.1875
- expert_ids: int32 [96, 4, 2], P('tp'), may hold values from 0 to 15, all different within a row
- gate_weight: bfloat16 [45056, 1024], P(('seq', 'tp')), may hold values from -0.1875 to 0.1875
- up_weight: bfloat16 [45056, 1024], P(('seq', 'tp')), may hold values from -0.1875 to 0.1875
- down_weight: bfloat16 [45056, 1024], P(('seq', 'tp')), may hold values from -0.109375 to 0.109375
Outputs:
- attn_out: bfloat16 [96, 4, 1024], P('tp', None, 'seq')
- layer_out: bfloat16 [96, 4, 1024], P('tp', None, 'seq')
Inputs may be any that keep to these rules, and one draw needn't show every extreme that they name: `lengths`: each length is 4096 or between 64 and 128; some request has 4096.
All inputs are finite; a program needn't handle non-finite values.
Results may differ from a plain program's by a relative error of at most 0.014.
Values may be sent and summed in bfloat16 or wider, within the bound.
A program may use at most 64 MiB of HBM per device.

v0:
```python
import jax
import jax.numpy as jnp
from jax import lax
from jax.sharding import PartitionSpec as P

HEADS = 16
masked_score = -1e30
norm_epsilon = 1e-06


def entering(part, axis, combine, identity):
    place = lax.axis_index(axis)
    gathered = lax.all_gather(part, axis)
    state = jnp.zeros_like(part) + jnp.asarray(identity, part.dtype)

    def one(turn, state):
        return combine(state, lax.dynamic_index_in_dim(gathered, turn, 0, False))

    return lax.fori_loop(0, place, one, state)


def add_counts(former, latter):
    return former + latter


def pick_slot(chosen_ids, earlier):
    onehot = chosen_ids[..., None] == jnp.arange(earlier.shape[2], dtype=jnp.int32)
    return jnp.sum(jnp.where(onehot, earlier[:, :, None, :], 0), axis=3)


def body(
    hidden_in,
    new_query,
    new_key,
    new_value,
    key_cache,
    value_cache,
    lengths,
    out_weight,
    norm_gain,
    router_weight,
    expert_ids,
    gate_weight,
    up_weight,
    down_weight,
):
    req_dev, steps, width = hidden_in.shape
    block = key_cache.shape[1]
    head_size = width // HEADS
    scale = head_size ** (-0.5)
    seq_index = lax.axis_index("seq")
    tp_index = lax.axis_index("tp")
    seq_size = lax.axis_size("seq")
    tp_size = lax.axis_size("tp")
    queries = new_query.reshape(req_dev, steps, HEADS, head_size)
    cache_keys = key_cache.reshape(req_dev, block, HEADS, head_size)
    cache_values = value_cache.reshape(req_dev, block, HEADS, head_size)
    fresh_keys = new_key.reshape(req_dev, steps, HEADS, head_size)
    fresh_values = new_value.reshape(req_dev, steps, HEADS, head_size)
    scores = (
        jnp.einsum("rthe,rphe->rhtp", queries, cache_keys, preferred_element_type=jnp.float32)
        * scale
    )
    positions = seq_index * block + jnp.arange(block, dtype=jnp.int32)
    usable = (positions[None, :] < lengths[:, None])[:, None, None, :]
    scores = jnp.where(usable, scores, masked_score)
    fresh_scores = (
        jnp.einsum("rthe,rshe->rhts", queries, fresh_keys, preferred_element_type=jnp.float32)
        * scale
    )
    causal = (jnp.arange(steps)[:, None] >= jnp.arange(steps)[None, :]) & (seq_index == 0)
    fresh_scores = jnp.where(causal, fresh_scores, masked_score)
    local_max = jnp.maximum(jnp.max(scores, axis=3), jnp.max(fresh_scores, axis=3))
    weights = jnp.where(usable, jnp.exp(scores - local_max[..., None]), 0.0)
    fresh_weights = jnp.where(causal, jnp.exp(fresh_scores - local_max[..., None]), 0.0)
    totals = jnp.sum(weights, axis=3) + jnp.sum(fresh_weights, axis=3)
    gathered_values = jnp.einsum(
        "rhtp,rphe->rhte",
        weights.astype(jnp.bfloat16),
        cache_values,
        preferred_element_type=jnp.float32,
    )
    gathered_values = gathered_values + jnp.einsum(
        "rhts,rshe->rhte",
        fresh_weights.astype(jnp.bfloat16),
        fresh_values,
        preferred_element_type=jnp.float32,
    )
    overall = lax.pmax(local_max, "seq")
    factors = jnp.exp(local_max - overall)
    totals, gathered_values = (
        lax.psum((totals * factors).astype(jnp.bfloat16), "seq").astype(jnp.float32),
        lax.psum((gathered_values * factors[..., None]).astype(jnp.bfloat16), "seq").astype(
            jnp.float32
        ),
    )
    context = (
        (gathered_values / totals[..., None])
        .transpose(0, 2, 1, 3)
        .reshape(req_dev, steps, width)
        .astype(jnp.bfloat16)
    )
    attention = jnp.einsum("rtd,de->rte", context, out_weight, preferred_element_type=jnp.float32)
    feature_block = width // seq_size
    attn_out = lax.dynamic_slice_in_dim(
        attention, seq_index * feature_block, feature_block, 2
    ).astype(jnp.bfloat16)
    residual = hidden_in.astype(jnp.float32) + attention
    normed = (
        residual
        * lax.rsqrt(jnp.mean(residual * residual, axis=-1, keepdims=True) + norm_epsilon)
        * norm_gain
    ).astype(jnp.bfloat16)
    experts = router_weight.shape[1]
    topk = expert_ids.shape[2]
    requests = req_dev * tp_size
    capacity = (5 * requests * topk + 4 * experts - 1) // (4 * experts)
    expert_range = jnp.arange(experts, dtype=jnp.int32)
    local_hits = jnp.sum((expert_ids[..., None] == expert_range).astype(jnp.int32), axis=2)
    counts = jnp.sum(local_hits, axis=0)
    before = entering(counts, "tp", add_counts, jnp.zeros_like(counts))
    earlier = (before[None] + jnp.cumsum(local_hits, axis=0) - local_hits).astype(jnp.int32)
    routing = jnp.concatenate([expert_ids, pick_slot(expert_ids, earlier)], axis=2)
    all_routing = lax.all_gather(routing, "tp", axis=0, tiled=True)
    all_ids = all_routing[:, :, :topk]
    all_slots = all_routing[:, :, topk:]
    all_normed = lax.all_gather(normed, "tp", axis=0, tiled=True)
    logits = jnp.einsum(
        "rtd,de->rte", all_normed, router_weight, preferred_element_type=jnp.float32
    )
    onehot = all_ids[..., None] == expert_range
    chosen = jnp.sum(jnp.where(onehot, logits[:, :, None, :], 0.0), axis=3)
    share = 1.0 / (1.0 + jnp.exp(chosen[:, :, ::-1] - chosen))
    slices = seq_size * tp_size // experts
    mine = (seq_index * tp_size + tp_index) // slices
    match = all_ids == mine
    slot_mine = jnp.sum(jnp.where(match, all_slots, 0), axis=2)
    share_mine = jnp.sum(jnp.where(match, share, 0.0), axis=2)
    kept = jnp.any(match, axis=2) & (slot_mine < capacity)
    select = kept[None] & (slot_mine[None] == jnp.arange(capacity, dtype=jnp.int32)[:, None, None])
    buffer = (
        jnp.einsum(
            "crt,rtd->tcd",
            select.astype(jnp.bfloat16),
            all_normed,
            preferred_element_type=jnp.float32,
        )
        .astype(jnp.bfloat16)
        .reshape(steps * capacity, width)
    )
    contract = (((1,), (1,)), ((), ()))
    gate = lax.dot_general(buffer, gate_weight, contract, preferred_element_type=jnp.float32)
    upward = lax.dot_general(buffer, up_weight, contract, preferred_element_type=jnp.float32)
    inner = (jax.nn.gelu(gate) * upward).astype(jnp.bfloat16)
    produced = jnp.dot(inner, down_weight, preferred_element_type=jnp.float32)
    placed = select.astype(jnp.float32) * share_mine[None]
    term = jnp.einsum(
        "crt,tcd->rtd",
        placed,
        produced.reshape(steps, capacity, width),
        precision=lax.Precision.HIGHEST,
    )
    row_sums = lax.psum_scatter(term.astype(jnp.bfloat16), "tp", scatter_dimension=0, tiled=True)
    mixture = lax.psum_scatter(row_sums, "seq", scatter_dimension=2, tiled=True).astype(jnp.float32)
    own_residual = lax.dynamic_slice_in_dim(residual, seq_index * feature_block, feature_block, 2)
    layer_out = (own_residual + mixture).astype(jnp.bfloat16)
    return (attn_out, layer_out)


def solution(mesh):
    return jax.shard_map(
        body,
        mesh=mesh,
        in_specs=(
            P("tp", None, None),
            P("tp", None, None),
            P("tp", None, None),
            P("tp", None, None),
            P("tp", "seq", None),
            P("tp", "seq", None),
            P("tp"),
            P(),
            P(),
            P(),
            P("tp", None, None),
            P(("seq", "tp"), None),
            P(("seq", "tp"), None),
            P(("seq", "tp"), None),
        ),
        out_specs=(P("tp", None, "seq"), P("tp", None, "seq")),
        check_vma=False,
    )
```

profile of v0, /device:TPU:0, one launch (start us, length us, event | category | flops | bytes accessed | tf_op | source)
XLA Modules:
  0.0 284.9 jit_solution(4095929092177931425)
XLA Ops:
  7.2 0.0 copy-start
  7.2 0.0 all-reduce.4.cloned.1.call-start
  7.2 1.0 reshape.92
  8.2 0.0 copy-start.3
  8.2 0.0 copy-start.6
  8.2 8.7 %copy.131 = bf16[3,1024,1024]{1,2,0:T(8,128)(2,1)} copy(bf16[3,1024,1024]{2,1,0:T(8,128)(2,1)} %param.20) | data formatting | bytes 12582912 | tf_op args[4]
  16.9 0.0 copy-done.3
  16.9 0.1 reshape.94
  17.0 0.2 fusion.30
  17.2 0.1 copy.135
  17.3 0.1 fusion.43
  17.5 0.1 copy.136
  17.6 0.0 copy-done.6
  17.6 0.1 broadcast_compare_fusion
  17.6 3.8 %fusion.61 = (f32[3,16,4]{2,1,0:T(8,128)S(1)}, f32[3,16,4,1024]{3,2,1,0:T(4,128)S(1)}) fusion(bf16[3,1024,16,64]{1,3,2,0:T(8,128)(2,1)} %bitcast.35, bf16[3,4,16,64]{3,2,1,0:T(8,128)(2,1)S(1)} %reshape.92, pred[3,1024]{1,0:T(4,128)(4,1)S(1)} %broadcast_compare_fusion), kind=kOutput, calls=%fused_computation.93 | convolution fusion | flops 25755456 | bytes 7106304 | tf_op jit(solution)/shard_map/rthe,rphe->rhtp/dot_general | solution.py:61
  21.4 0.1 copy.138
  21.5 17.1 %pmax.7 = f32[3,16,4]{2,1,0:T(8,128)S(1)} all-reduce(f32[3,16,4]{2,1,0:T(8,128)S(1)} %max.9), channel_id=1, replica_groups=mesh['seq'=4,'tp'=32] {'seq'}, use_global_device_ids=true, to_apply=%region_2.3 | all-reduce | flops 192 | bytes 1536 | tf_op jit(solution)/shard_map/pmax | solution.py:89
  38.6 0.5 fusion.12
  39.1 0.1 fusion.50
  39.2 0.1 copy.141
  39.3 8.6 %copy.137 = bf16[3,1024,1024]{1,2,0:T(8,128)(2,1)} copy(bf16[3,1024,1024]{2,1,0:T(8,128)(2,1)} %param.21) | data formatting | bytes 12582912 | tf_op args[5]
  48.0 0.0 copy-start.7
  48.0 4.6 %fusion.14 = f32[3,16,4,64]{3,2,1,0:T(4,128)S(1)} fusion(bf16[3,1024,16,64]{1,3,2,0:T(8,128)(2,1)} %bitcast.36, f32[3,16,4,1024]{3,2,1,0:T(4,128)S(1)} %get-tuple-element.49, f32[3,16,4]{2,1,0:T(8,128)S(1)} %max.9, pred[3,1024]{1,0:T(4,128)(4,1)S(1)} %broadcast_compare_fusion), kind=kOutput, calls=%fused_computation.22 | convolution fusion | flops 25755648 | bytes 7130880 | tf_op jit(solution)/shard_map/rhtp,rphe->rhte/dot_general | solution.py:77
  52.6 0.2 copy.139
  52.8 0.0 copy-done.4
  52.8 0.1 reshape.96
  52.9 0.2 fusion.5
  53.1 14.9 %all-reduce.1 = (bf16[3,16,4,64]{3,2,1,0:T(4,128)(2,1)S(1)}, bf16[3,16,4]{2,1,0:T(8,128)(2,1)S(1)}) all-reduce(bf16[3,16,4,64]{3,2,1,0:T(4,128)(2,1)S(1)} %fusion.5, bf16[3,16,4]{2,1,0:T(8,128)(2,1)S(1)} %get-tuple-element.42), channel_id=1, replica_groups=mesh['seq'=4,'tp'=32] {'seq'}, use_global_device_ids=true, to_apply=%region_3.4 | all-reduce | flops 12480 | bytes 49920 | tf_op jit(solution)/shard_map/psum | solution.py:93
  68.0 0.1 fusion.28
  68.2 0.1 convert_element_type.67
  68.3 0.0 copy-done
  68.3 0.0 copy-done.2
  68.3 0.5 multiply_reduce_fusion
  68.8 0.0 copy-done.5
  68.8 0.1 multiply_convert_fusion
  68.9 26.4 %all_gather.15 = bf16[96,4,1024]{2,1,0:T(4,128)(2,1)S(1)} all-gather(bf16[3,4,1024]{2,1,0:T(4,128)(2,1)S(1)} %multiply_convert_fusion), channel_id=1, replica_groups=mesh['seq'=4,'tp'=32] {'tp'}, dimensions={0}, use_global_device_ids=true | all-gather | bytes 811008 | tf_op jit(solution)/shard_map/all_gather | solution.py:127
  95.3 0.1 convert_reduce_fusion.1
  95.3 23.6 %all-gather.1 = s32[32,4,16]{2,1,0:T(4,128)S(1)} all-gather(s32[1,4,16]{2,1,0:T(4,128)S(1)} %bitcast.39), channel_id=2, replica_groups=mesh['seq'=4,'tp'=32] {'tp'}, dimensions={0}, use_global_device_ids=true | all-gather | bytes 8448 | tf_op jit(solution)/shard_map/all_gather | solution.py:13
  119.0 0.3 select_reduce_fusion.1
  119.2 0.1 copy.143
  119.3 23.6 %all_gather.14 = s32[96,4,4]{2,1,0:T(4,128)S(1)} all-gather(s32[3,4,4]{2,1,0:T(4,128)S(1)} %copy.143), channel_id=1, replica_groups=mesh['seq'=4,'tp'=32] {'tp'}, dimensions={0}, use_global_device_ids=true | all-gather | bytes 6336 | tf_op jit(solution)/shard_map/all_gather | solution.py:124
  142.9 0.2 fusion.60
  143.1 0.1 copy.161
  143.2 0.4 fusion.9
  143.7 0.1 copy.162
  143.8 0.1 fusion.52
  143.9 0.5 convolution_convert_fusion.1
  144.5 1.5 fusion.62
  145.9 2.0 fusion.7
  148.0 1.4 fusion.2
  149.4 1.5 copy.155
  150.9 0.0 all-reduce.4.cloned.1.call-update
  150.9 0.0 reduce-scatter.4.cloned.1.call-start
  151.0 0.6 dynamic-slice
  152.2 101.1 %all-reduce.4.cloned.1.call-done = bf16[96,4,1024]{2,1,0:T(4,128)(2,1)} async-done(((bf16[96,4,1024]{2,1,0:T(4,128)(2,1)}), bf16[96,4,1024]{2,1,0:T(4,128)(2,1)}) %all-reduce.4.cloned.1.call-update) | async-done | bytes 786448
  253.3 0.7 constant_dynamic-slice_fusion
  254.1 0.7 copy.156
  254.8 1.2 reshape.105
  256.0 0.0 reduce-scatter.4.cloned.1.call-update
  256.0 0.6 dynamic-slice_convert_fusion
  256.6 19.6 %reduce-scatter.4.cloned.1.call-done = bf16[256,12]{1,0:T(8,128)(2,1)} async-done(((bf16[1024,12]{1,0:T(8,128)(2,1)}), bf16[256,12]{1,0:T(8,128)(2,1)}) %reduce-scatter.4.cloned.1.call-update) | async-done | bytes 6160
  276.3 1.0 reshape.106
  277.2 0.2 copy.157
  277.4 0.6 add_convert_fusion
  (26 shorter events, 0.3 us)
Async XLA Ops:
  7.2 61.1 %copy-start = (bf16[1024,1024]{1,0:T(8,128)(2,1)S(1)}, bf16[1024,1024]{1,0:T(8,128)(2,1)}, u32[]{:S(2)}) copy-start(bf16[1024,1024]{1,0:T(8,128)(2,1)} %param.23) | copy-start | bytes 6291460
  7.2 246.2 %all-reduce.4.cloned.1.call-start = ((), (), s32[]{:S(2)}) async-start(), calls=%async_computation.2 | async-start | bytes 1572864
  8.2 8.7 %copy-start.3 = (bf16[3,4,1024]{2,1,0:T(4,128)(2,1)S(1)}, bf16[3,4,1024]{2,1,0:T(4,128)(2,1)}, u32[]{:S(2)}) copy-start(bf16[3,4,1024]{2,1,0:T(4,128)(2,1)} %param.18) | copy-start | bytes 73732
  8.2 9.3 %copy-start.6 = (s32[3]{0:T(128)S(1)}, s32[3]{0:T(128)}, u32[]{:S(2)}) copy-start(s32[3]{0:T(128)} %param.22) | copy-start | bytes 40
  48.0 4.8 %copy-start.4 = (bf16[3,4,1024]{2,1,0:T(4,128)(2,1)S(1)}, bf16[3,4,1024]{2,1,0:T(4,128)(2,1)}, u32[]{:S(2)}) copy-start(bf16[3,4,1024]{2,1,0:T(4,128)(2,1)} %param.19) | copy-start | bytes 73732
  48.0 20.3 %copy-start.2 = (bf16[3,4,1024]{2,1,0:T(4,128)(2,1)S(1)}, bf16[3,4,1024]{2,1,0:T(4,128)(2,1)}, u32[]{:S(2)}) copy-start(bf16[3,4,1024]{2,1,0:T(4,128)(2,1)} %param.16) | copy-start | bytes 73732
  48.0 20.8 %copy-start.5 = (f32[1024]{0:T(1024)S(1)}, f32[1024]{0:T(1024)}, u32[]{:S(2)}) copy-start(f32[1024]{0:T(1024)} %param.24) | copy-start | bytes 12292
  48.0 47.3 %copy-start.1 = (s32[3,4,2]{1,2,0:T(2,128)S(1)}, s32[3,4,2]{1,2,0:T(2,128)}, u32[]{:S(2)}) copy-start(s32[3,4,2]{1,2,0:T(2,128)} %param.26) | copy-start | bytes 292
  48.0 95.2 %copy-start.7 = (bf16[1024,16]{0,1:T(8,128)(2,1)S(1)}, bf16[1024,16]{0,1:T(8,128)(2,1)}, u32[]{:S(2)}) copy-start(bf16[1024,16]{0,1:T(8,128)(2,1)} %param.25) | copy-start | bytes 98308
  68.8 82.2 %copy-start.8 = (u32[128]{0:T(128)S(1)}, u32[128]{0:T(128)}, u32[]{:S(2)}) copy-start(u32[128]{0:T(128)} %constant.85) | copy-start | bytes 1540
  150.9 125.3 %reduce-scatter.4.cloned.1.call-start = ((), (), s32[]{:S(2)}) async-start(), calls=%async_computation.1 | async-start | bytes 327680
Sparse Core Ops, SparseCore 0:
  151.1 102.2 all-reduce.3
  256.1 20.0 reduce-scatter.3
where the time goes:
time: 286 us; the launch traced here: 285 us
  waiting for transfers between devices  121 us (42%)
  blocking collectives  106 us (37%)
  local copies, waits for them, and re-layouts  26.3 us (9%)
  matrix products  15.1 us (5%)
  between operations  15 us (5%)
    unnamed x4, waiting for transfers between devices  121 us
    all_gather x1, blocking collectives, body(): all_normed = lax.all_gather(normed, 'tp', axis=0, tiled=True)  26.4 us
    all_gather x1, blocking collectives, entering(): gathered = lax.all_gather(part, axis)  23.6 us
    all_gather x1, blocking collectives, body(): all_routing = lax.all_gather(routing, 'tp', axis=0, tiled=True)  23.6 us
    unnamed x28, local copies, waits for them, and re-layouts  21.9 us
    pmax x1, blocking collectives, body(): overall = lax.pmax(local_max, 'seq')  17.1 us
    psum x1, blocking collectives, body(): lax.psum((gathered_values * factors[..., None]).astype(jnp.bfloat16), 'seq')  14.9 us
  transfers between devices with their start and end apart: 2, of which 2 were waited for; matrix products, arithmetic and copies ran while one was open for 0% of the time, Pallas kernels for 0%

commit v1 on v0

--- a/solution.py
+++ b/solution.py
@@ -121,7 +121,9 @@
     before = entering(counts, "tp", add_counts, jnp.zeros_like(counts))
     earlier = (before[None] + jnp.cumsum(local_hits, axis=0) - local_hits).astype(jnp.int32)
     routing = jnp.concatenate([expert_ids, pick_slot(expert_ids, earlier)], axis=2)
-    all_routing = lax.all_gather(routing, "tp", axis=0, tiled=True)
+    all_routing = jnp.concatenate(
+        lax.all_to_all(jnp.stack([routing] * lax.axis_size("tp")), "tp", 0, 0), axis=0
+    )
     all_ids = all_routing[:, :, :topk]
     all_slots = all_routing[:, :, topk:]
     all_normed = lax.all_gather(normed, "tp", axis=0, tiled=True)

time: 286 us -> 274 us (0.958)
  blocking collectives: 106 us -> 83 us
  starting transfers between devices: 0.08 us -> 6.29 us
  other arithmetic: 2.15 us -> 5.13 us
    all_gather x1 -> x0, blocking collectives: 23.6 us -> none  [body(): all_routing = lax.all_gather(routing, 'tp', axis=0, tiled=True)]
    all_to_all x0 -> x1, starting transfers between devices: none -> 6.2 us  [body(): lax.all_to_all(jnp.stack([routing] * lax.axis_size('tp')), 'tp', 0, 0)]
    unnamed x28 -> x26, local copies, waits for them, and re-layouts: 21.9 us -> 21.9 us
  transfers between devices with their start and end apart: 2 -> 3, of which waited for: 2 -> 2; matrix products, arithmetic and copies ran while one was open for 0% -> 12% of each run, Pallas kernels for 0% -> 0%
where the time goes in v1:
time: 274 us; the launch traced here: 273 us
  waiting for transfers between devices  121 us (44%)
  blocking collectives  83 us (30%)
  local copies, waits for them, and re-layouts  26.9 us (10%)
  matrix products  15.7 us (6%)
  between operations  15 us (5%)
  starting transfers between devices  6.29 us (2%)
  other arithmetic  5.13 us (2%)
    unnamed x4, waiting for transfers between devices  121 us
    all_gather x1, blocking collectives, entering(): gathered = lax.all_gather(part, axis)  25.7 us
    all_gather x1, blocking collectives, body(): all_normed = lax.all_gather(normed, 'tp', axis=0, tiled=True)  25.4 us
    unnamed x26, local copies, waits for them, and re-layouts  21.9 us
    pmax x1, blocking collectives, body(): overall = lax.pmax(local_max, 'seq')  17 us
    psum x1, blocking collectives, body(): lax.psum((gathered_values * factors[..., None]).astype(jnp.bfloat16), 'seq')  14.9 us
    all_to_all x1, starting transfers between devices, body(): lax.all_to_all(jnp.stack([routing] * lax.axis_size('tp')), 'tp', 0, 0)  6.2 us
  transfers between devices with their start and end apart: 3, of which 2 were waited for; matrix products, arithmetic and copies ran while one was open for 12% of the time, Pallas kernels for 0%

profile of v1, /device:TPU:0, one launch (start us, length us, event | category | flops | bytes accessed | tf_op | source)
XLA Modules:
  0.0 272.6 jit_solution(218410968666054528)
XLA Ops:
  7.2 0.0 copy-start
  7.2 0.9 convert_reduce_fusion.1
  8.1 25.7 %all-gather.1 = s32[32,4,16]{2,1,0:T(4,128)S(1)} all-gather(s32[1,4,16]{2,1,0:T(4,128)S(1)} %bitcast.41), channel_id=2, replica_groups=mesh['seq'=4,'tp'=32] {'tp'}, dimensions={0}, use_global_device_ids=true | all-gather | bytes 8448 | tf_op jit(solution)/shard_map/all_gather | solution.py:13
  33.9 0.9 select_reduce_fusion.1
  34.8 0.7 pad_add_fusion
  35.5 0.1 copy.153
  35.6 0.7 stack.2
  36.3 6.2 %all-to-all-start = ((s32[32,3,4,4]{3,2,1,0:T(4,128)}), s32[32,3,4,4]{3,2,1,0:T(4,128)S(1)}, u32[]{:S(2)}, u32[]{:S(2)}) async-start(s32[32,3,4,4]{3,2,1,0:T(4,128)} %stack.2), calls=%async_computation | async-start | bytes 393216 | tf_op jit(solution)/shard_map/all_to_all | solution.py:125
  42.5 0.0 all-reduce.4.cloned.1.call-start
  42.6 0.8 reshape.97
  43.4 0.0 copy-start.2
  43.4 0.0 copy-start.5
  43.5 8.7 %copy.141 = bf16[3,1024,1024]{1,2,0:T(8,128)(2,1)} copy(bf16[3,1024,1024]{2,1,0:T(8,128)(2,1)} %param.20) | data formatting | bytes 12582912 | tf_op args[4]
  52.1 0.0 copy-done.2
  52.1 0.1 reshape.99
  52.2 0.2 fusion.30
  52.4 0.1 copy.145
  52.5 0.1 fusion.43
  52.7 0.1 copy.146
  52.8 0.1 broadcast_compare_fusion
  52.8 3.8 %fusion.61 = (f32[3,16,4]{2,1,0:T(8,128)S(1)}, f32[3,16,4,1024]{3,2,1,0:T(4,128)S(1)}) fusion(bf16[3,1024,16,64]{1,3,2,0:T(8,128)(2,1)} %bitcast.36, bf16[3,4,16,64]{3,2,1,0:T(8,128)(2,1)S(1)} %reshape.97, pred[3,1024]{1,0:T(4,128)(4,1)S(1)} %broadcast_compare_fusion), kind=kOutput, calls=%fused_computation.93 | convolution fusion | flops 25755456 | bytes 7106304 | tf_op jit(solution)/shard_map/rthe,rphe->rhtp/dot_general | solution.py:61
  56.6 0.1 copy.148
  56.7 17.0 %pmax.7 = f32[3,16,4]{2,1,0:T(8,128)S(1)} all-reduce(f32[3,16,4]{2,1,0:T(8,128)S(1)} %max.9), channel_id=1, replica_groups=mesh['seq'=4,'tp'=32] {'seq'}, use_global_device_ids=true, to_apply=%region_2.3 | all-reduce | flops 192 | bytes 1536 | tf_op jit(solution)/shard_map/pmax | solution.py:89
  73.8 0.5 fusion.12
  74.2 0.1 fusion.50
  74.3 0.1 copy.151
  74.4 8.6 %copy.147 = bf16[3,1024,1024]{1,2,0:T(8,128)(2,1)} copy(bf16[3,1024,1024]{2,1,0:T(8,128)(2,1)} %param.21) | data formatting | bytes 12582912 | tf_op args[5]
  83.1 4.6 %fusion.14 = f32[3,16,4,64]{3,2,1,0:T(4,128)S(1)} fusion(bf16[3,1024,16,64]{1,3,2,0:T(8,128)(2,1)} %bitcast.37, f32[3,16,4,1024]{3,2,1,0:T(4,128)S(1)} %get-tuple-element.49, f32[3,16,4]{2,1,0:T(8,128)S(1)} %max.9, pred[3,1024]{1,0:T(4,128)(4,1)S(1)} %broadcast_compare_fusion), kind=kOutput, calls=%fused_computation.22 | convolution fusion | flops 25755648 | bytes 7130880 | tf_op jit(solution)/shard_map/rhtp,rphe->rhte/dot_general | solution.py:77
  87.7 0.2 copy.149
  87.9 0.1 reshape.101
  88.0 0.2 fusion.5
  88.2 14.9 %all-reduce.1 = (bf16[3,16,4,64]{3,2,1,0:T(4,128)(2,1)S(1)}, bf16[3,16,4]{2,1,0:T(8,128)(2,1)S(1)}) all-reduce(bf16[3,16,4,64]{3,2,1,0:T(4,128)(2,1)S(1)} %fusion.5, bf16[3,16,4]{2,1,0:T(8,128)(2,1)S(1)} %get-tuple-element.42), channel_id=1, replica_groups=mesh['seq'=4,'tp'=32] {'seq'}, use_global_device_ids=true, to_apply=%region_3.4 | all-reduce | flops 12480 | bytes 49920 | tf_op jit(solution)/shard_map/psum | solution.py:93
  103.1 0.1 fusion.28
  103.3 0.1 convert_element_type.67
  103.4 0.0 copy-done
  103.4 0.0 copy-start.7
  103.4 0.5 multiply_reduce_fusion
  103.9 0.1 multiply_convert_fusion
  104.0 25.4 %all_gather.11 = bf16[96,4,1024]{2,1,0:T(4,128)(2,1)S(1)} all-gather(bf16[3,4,1024]{2,1,0:T(4,128)(2,1)S(1)} %multiply_convert_fusion), channel_id=1, replica_groups=mesh['seq'=4,'tp'=32] {'tp'}, dimensions={0}, use_global_device_ids=true | all-gather | bytes 811008 | tf_op jit(solution)/shard_map/all_gather | solution.py:129
  129.4 1.0 fusion.9
  130.4 0.0 all-to-all-done
  130.4 0.2 fusion.60
  130.5 0.1 copy.167
  130.6 0.8 select_reduce_fusion
  131.5 0.1 copy.168
  131.6 0.1 fusion.52
  131.7 0.5 convolution_convert_fusion.1
  132.3 1.5 fusion.62
  133.7 2.0 fusion.7
  135.8 1.4 fusion.2
  137.2 1.5 copy.160
  138.7 0.0 all-reduce.4.cloned.1.call-update
  138.8 0.0 reduce-scatter.4.cloned.1.call-start
  138.8 0.6 dynamic-slice
  140.1 101.0 %all-reduce.4.cloned.1.call-done = bf16[96,4,1024]{2,1,0:T(4,128)(2,1)} async-done(((bf16[96,4,1024]{2,1,0:T(4,128)(2,1)}), bf16[96,4,1024]{2,1,0:T(4,128)(2,1)}) %all-reduce.4.cloned.1.call-update) | async-done | bytes 786448
  241.1 0.7 constant_dynamic-slice_fusion
  241.8 0.7 copy.162
  242.6 1.2 reshape.111
  243.8 0.0 reduce-scatter.4.cloned.1.call-update
  243.8 0.6 dynamic-slice_convert_fusion
  244.4 19.6 %reduce-scatter.4.cloned.1.call-done = bf16[256,12]{1,0:T(8,128)(2,1)} async-done(((bf16[1024,12]{1,0:T(8,128)(2,1)}), bf16[256,12]{1,0:T(8,128)(2,1)}) %reduce-scatter.4.cloned.1.call-update) | async-done | bytes 6160
  264.0 1.0 reshape.112
  265.0 0.2 copy.163
  265.2 0.6 add_convert_fusion
  (26 shorter events, 0.2 us)
Async XLA Ops:
  7.2 96.2 %copy-start = (bf16[1024,1024]{1,0:T(8,128)(2,1)S(1)}, bf16[1024,1024]{1,0:T(8,128)(2,1)}, u32[]{:S(2)}) copy-start(bf16[1024,1024]{1,0:T(8,128)(2,1)} %param.23) | copy-start | bytes 6291460
  36.3 94.1 %all-to-all-start = ((s32[32,3,4,4]{3,2,1,0:T(4,128)}), s32[32,3,4,4]{3,2,1,0:T(4,128)S(1)}, u32[]{:S(2)}, u32[]{:S(2)}) async-start(s32[32,3,4,4]{3,2,1,0:T(4,128)} %stack.2), calls=%async_computation | async-start | bytes 393216 | tf_op jit(solution)/shard_map/all_to_all | solution.py:125
  42.5 198.6 %all-reduce.4.cloned.1.call-start = ((), (), s32[]{:S(2)}) async-start(), calls=%async_computation.3 | async-start | bytes 1572864
  43.4 8.7 %copy-start.2 = (bf16[3,4,1024]{2,1,0:T(4,128)(2,1)S(1)}, bf16[3,4,1024]{2,1,0:T(4,128)(2,1)}, u32[]{:S(2)}) copy-start(bf16[3,4,1024]{2,1,0:T(4,128)(2,1)} %param.18) | copy-start | bytes 73732
  43.4 9.3 %copy-start.5 = (s32[3]{0:T(128)S(1)}, s32[3]{0:T(128)}, u32[]{:S(2)}) copy-start(s32[3]{0:T(128)} %param.22) | copy-start | bytes 40
  83.1 4.8 %copy-start.3 = (bf16[3,4,1024]{2,1,0:T(4,128)(2,1)S(1)}, bf16[3,4,1024]{2,1,0:T(4,128)(2,1)}, u32[]{:S(2)}) copy-start(bf16[3,4,1024]{2,1,0:T(4,128)(2,1)} %param.19) | copy-start | bytes 73732
  83.1 20.3 %copy-start.1 = (bf16[3,4,1024]{2,1,0:T(4,128)(2,1)S(1)}, bf16[3,4,1024]{2,1,0:T(4,128)(2,1)}, u32[]{:S(2)}) copy-start(bf16[3,4,1024]{2,1,0:T(4,128)(2,1)} %param.16) | copy-start | bytes 73732
  83.1 20.8 %copy-start.4 = (f32[1024]{0:T(1024)S(1)}, f32[1024]{0:T(1024)}, u32[]{:S(2)}) copy-start(f32[1024]{0:T(1024)} %param.24) | copy-start | bytes 12292
  83.1 46.3 %copy-start.6 = (bf16[1024,16]{0,1:T(8,128)(2,1)S(1)}, bf16[1024,16]{0,1:T(8,128)(2,1)}, u32[]{:S(2)}) copy-start(bf16[1024,16]{0,1:T(8,128)(2,1)} %param.25) | copy-start | bytes 98308
  103.4 35.4 %copy-start.7 = (u32[128]{0:T(128)S(1)}, u32[128]{0:T(128)}, u32[]{:S(2)}) copy-start(u32[128]{0:T(128)} %constant.85) | copy-start | bytes 1540
  138.8 125.3 %reduce-scatter.4.cloned.1.call-start = ((), (), s32[]{:S(2)}) async-start(), calls=%async_computation.2 | async-start | bytes 327680
Sparse Core Ops, SparseCore 0:
  138.9 102.1 all-reduce.3
  243.9 20.0 reduce-scatter.3
